TPU v7x, 256 devices: a whole 4x4x8 slice. The times are simulated.
256 devices in a mesh: dp: 4 (over y), space: 64 (over z, x, core).
Axes of the slice: x: 4, y: 4, z: 8, core: 2. Of those that a mesh axis runs over, the one named last changes fastest.
Arguments:
- features: bfloat16 [4, 128, 8, 8, 8, 128], P('dp', 'space'), may hold values from -6 to 6
- occupancy: int32 [4, 128, 8, 8, 8], P('dp', 'space'), may hold values from 0 to 1
- neighbours: int32 [4, 128, 26], P('dp', 'space'), may hold values from -1 to 127, as said below
- weight: bfloat16 [27, 128, 128], replicated, may hold values from -0.109375 to 0.109375
- cotangent: bfloat16 [4, 128, 8, 8, 8, 128], P('dp', 'space'), may hold values from -6 to 6
Outputs:
- response: bfloat16 [4, 128, 8, 8, 8, 128], P('dp', 'space')
- grad_input: bfloat16 [4, 128, 8, 8, 8, 128], P('dp', 'space')
- grad_weight: float32 [3456, 128], P('space')
Inputs may be any that keep to these rules, and one draw needn't show every extreme that they name: `neighbours`: A scan's blocks sit in a coarse grid of 64 slabs along the first dimension, each one cell thick and 4 cells across; each slab holds exactly 2 blocks, numbered slab by slab and inside a slab in the Morton order of their cells, so block g lies in slab g // 2; entry o of block g names the block in the adjacent cell in direction o, or -1 if that cell is empty or outside the grid; the relation is symmetric.
All inputs are finite; a program needn't handle non-finite values.
Results may differ from a plain program's by a relative error of at most 0.001.
Values may be sent and summed in bfloat16 or wider, within the bound.
A program may use at most 64 MiB of HBM per device.

v0:
```python
import math
import jax
import jax.numpy as jnp
from jax import lax
from jax.sharding import PartitionSpec as P

directions = [
    (along_x, along_y, along_z)
    for along_x in (-1, 0, 1)
    for along_y in (-1, 0, 1)
    for along_z in (-1, 0, 1)
    if (along_x, along_y, along_z) != (0, 0, 0)
]
kernel_taps = [
    (along_x, along_y, along_z)
    for along_x in range(3)
    for along_y in range(3)
    for along_z in range(3)
]


def padded_2(block, sides, width):
    for axis, dim in sides:
        count = lax.axis_size(axis)
        forward = [(i, i + 1) for i in range(count - 1)]
        backward = [(target, source) for source, target in forward]
        low = lax.ppermute(
            lax.slice_in_dim(block, block.shape[dim] - width, None, axis=dim), axis, forward
        )
        high = lax.ppermute(lax.slice_in_dim(block, 0, width, axis=dim), axis, backward)
        block = jnp.concatenate([low, block, high], axis=dim)
    return block


def side_slices(offset, extent):
    chosen = []
    for stride in offset:
        if stride == 1:
            chosen.append(slice(extent - 1, extent))
        elif stride == -1:
            chosen.append(slice(0, 1))
        else:
            chosen.append(slice(0, extent))
    return tuple(chosen)


def rim_slices(offset, extent):
    chosen = []
    for stride in offset:
        if stride == 1:
            chosen.append(slice(extent + 1, extent + 2))
        elif stride == -1:
            chosen.append(slice(0, 1))
        else:
            chosen.append(slice(1, extent + 1))
    return tuple(chosen)


def end_planes(field):
    count = field.shape[0]
    extent = field.shape[1]
    return jnp.stack([field[:, 0], field[:, extent - 1]]).reshape(2, count, -1)


def fill_rims(field, arrived, links, position):
    count = field.shape[0]
    extent = field.shape[1]
    channels = field.shape[-1]
    zero_bf = jnp.zeros((), jnp.bfloat16)
    before = arrived[0].reshape(count, extent, extent, channels)
    after = arrived[3].reshape(count, extent, extent, channels)
    padded = jnp.pad(field, ((0, 0), (1, 1), (1, 1), (1, 1), (0, 0)))
    whole = (slice(None),)
    for slot_index, offset in enumerate(directions):
        opposite = tuple((-stride for stride in offset))
        if offset[0] == 0:
            source = field[whole + side_slices(opposite, extent)]
        elif offset[0] == -1:
            source = before[whole + side_slices(opposite[1:], extent)][:, None]
        else:
            source = after[whole + side_slices(opposite[1:], extent)][:, None]
        other = links[:, slot_index]
        local = other - (position + offset[0]) * count
        picked = jnp.take(source, jnp.clip(local, 0, count - 1), axis=0)
        picked = jnp.where((other >= 0)[:, None, None, None, None], picked, zero_bf)
        padded = padded.at[whole + rim_slices(offset, extent)].set(picked)
    return padded


def window_at(padded, start_x, start_y, start_z, extent, block_lo, block_hi):
    channels = padded.shape[-1]
    return padded[
        block_lo:block_hi,
        start_x : start_x + extent,
        start_y : start_y + extent,
        start_z : start_z + extent,
    ].reshape(-1, channels)


def forward_each(padded_x, flat_g, weight, extent):
    count = padded_x.shape[0]
    channels = padded_x.shape[-1]
    summed = jnp.zeros((count * extent**3, channels), jnp.float32)
    grads = []
    for number, (along_x, along_y, along_z) in enumerate(kernel_taps):
        window = window_at(padded_x, along_x, along_y, along_z, extent, 0, count)
        summed = summed + jnp.dot(window, weight[number], preferred_element_type=jnp.float32)
        grads.append(
            lax.dot_general(
                window, flat_g, (((0,), (0,)), ((), ())), preferred_element_type=jnp.float32
            )
        )
    return (summed, jnp.concatenate(grads, axis=0))


def backward_each(padded_g, weight, extent):
    count = padded_g.shape[0]
    channels = padded_g.shape[-1]
    summed = jnp.zeros((count * extent**3, channels), jnp.float32)
    for number, (along_x, along_y, along_z) in enumerate(kernel_taps):
        window = window_at(padded_g, 2 - along_x, 2 - along_y, 2 - along_z, extent, 0, count)
        summed = summed + lax.dot_general(
            window, weight[number], (((1,), (1,)), ((), ())), preferred_element_type=jnp.float32
        )
    return summed


def per_device(features, occupancy, neighbours, weight, cotangent):
    count = features.shape[1]
    extent = features.shape[2]
    channels = features.shape[-1]
    devices = lax.axis_size("space")
    scans_count = lax.axis_size("dp")
    position = lax.axis_index("space")
    zero_bf = jnp.zeros((), jnp.bfloat16)
    zero_f = jnp.zeros((), jnp.float32)
    active = occupancy[0][..., None] > 0
    masked = jnp.where(active, features[0], zero_bf)
    upstream = jnp.where(active, cotangent[0], zero_bf)
    links = neighbours[0]
    arrived_x = padded_2(end_planes(masked), (("space", 0),), 1)
    padded_x = fill_rims(masked, arrived_x, links, position)
    flat_g = upstream.reshape(-1, channels)
    forward_sum, kernel_grad = forward_each(padded_x, flat_g, weight, extent)
    response = jnp.where(
        active, forward_sum.reshape(count, extent, extent, extent, channels), zero_f
    ).astype(jnp.bfloat16)
    arrived_g = padded_2(end_planes(upstream), (("space", 0),), 1)
    padded_g = fill_rims(upstream, arrived_g, links, position)
    backward_sum = backward_each(padded_g, weight, extent)
    grad_input = jnp.where(
        active, backward_sum.reshape(count, extent, extent, extent, channels), zero_f
    ).astype(jnp.bfloat16)
    across_scans = lax.psum(kernel_grad, "dp")
    shard_rows = lax.psum_scatter(across_scans, "space", scatter_dimension=0, tiled=True)
    scale_factor = 1.0 / math.sqrt(scans_count * devices * count * extent**3)
    return (response[None], grad_input[None], shard_rows * scale_factor)


def solution(mesh):
    placed = (
        P("dp", "space", None, None, None, None),
        P("dp", "space", None, None, None),
        P("dp", "space", None),
        P(),
        P("dp", "space", None, None, None, None),
    )
    return jax.shard_map(
        per_device,
        mesh=mesh,
        in_specs=placed,
        out_specs=(
            P("dp", "space", None, None, None, None),
            P("dp", "space", None, None, None, None),
            P("space", None),
        ),
        check_vma=False,
    )
```

profile of v0, /device:TPU:6, one launch (start us, length us, event | category | flops | bytes accessed | tf_op | source)
XLA Modules:
  0.0 260.6 jit_solution(3344975392172040905)
XLA Ops:
  2.8 1.9 collective-permute-start
  4.7 3.8 %collective-permute-start.2 = (bf16[1,2,8192]{2,1,0:T(2,128)(2,1)S(1)}, bf16[1,2,8192]{2,1,0:T(2,128)(2,1)S(1)}, u32[]{:S(2)}, u32[]{:S(2)}) collective-permute-start(bf16[1,2,8192]{2,1,0:T(2,128)(2,1)S(1)} %slice.2775), channel_id=1, source_target_pairs={{0,1},{1,2},{2,3},{3,4},{4,5},{5,6},{6,7},{7,8},{8,9},{9,10},{10,1... | collective-permute-start | bytes 98312 | tf_op jit(solution)/shard_map/ppermute | solution.py:27
  8.6 1.9 collective-permute-start.3
  10.5 2.2 collective-permute-start.1
  14.0 1.9 compare_reduce_fusion
  61.0 1.4 scatter.194
  95.1 64.4 %fusion = f32[64,128]{1,0:T(8,128)S(1)} fusion(f32[3456,128]{1,0:T(8,128)} %fusion.1), kind=kCustom, calls=%all-reduce-scatter | all-reduce-scatter fusion | flops 524289 | bytes 1803264
  160.1 1.9 collective-permute-start.10
  162.0 4.2 %collective-permute-start.11 = (f32[64,128]{1,0:T(8,128)S(1)}, f32[64,128]{1,0:T(8,128)}, u32[]{:S(2)}, u32[]{:S(2)}) collective-permute-start(f32[64,128]{1,0:T(8,128)S(1)} %fusion), channel_id=1, source_target_pairs={{0,8},{1,9},{2,10},{3,11},{4,12},{5,13},{6,14},{7,15},{8,16},{9,17... | collective-permute-start | bytes 98312
  166.2 3.0 %collective-permute-start.12 = (f32[64,128]{1,0:T(8,128)S(1)}, f32[64,128]{1,0:T(8,128)}, u32[]{:S(2)}, u32[]{:S(2)}) collective-permute-start(f32[64,128]{1,0:T(8,128)S(1)} %fusion), channel_id=1, source_target_pairs={{0,9},{1,10},{2,11},{3,12},{4,13},{5,14},{6,15},{7,16},{8,17},{9,1... | collective-permute-start | bytes 98312
  169.2 3.3 %collective-permute-start.4 = (f32[64,128]{1,0:T(8,128)S(1)}, f32[64,128]{1,0:T(8,128)}, u32[]{:S(2)}, u32[]{:S(2)}) collective-permute-start(f32[64,128]{1,0:T(8,128)S(1)} %fusion), channel_id=1, source_target_pairs={{0,1},{1,2},{2,3},{3,4},{4,5},{5,6},{6,7},{7,8},{8,9},{9,10},{10,1... | collective-permute-start | bytes 98312
  172.5 1.4 fusion.184
  173.9 2.3 fusion.183
  184.6 2.0 scatter.236
  186.7 2.0 scatter.239
  199.3 3.9 %collective-permute-start.13 = (f32[54,128]{1,0:T(8,128)S(1)}, f32[54,128]{1,0:T(8,128)S(1)}, u32[]{:S(2)}, u32[]{:S(2)}) collective-permute-start(f32[54,128]{1,0:T(8,128)S(1)} %copy-done.22), channel_id=1, source_target_pairs={{0,10},{1,11},{2,12},{3,13},{4,14},{5,15},{6,16},{7,17},{8,18},{9,... | collective-permute-start | bytes 82952
  217.4 3.4 %collective-permute-start.5 = (f32[64,128]{1,0:T(8,128)S(1)}, f32[64,128]{1,0:T(8,128)S(1)}, u32[]{:S(2)}, u32[]{:S(2)}) collective-permute-start(f32[64,128]{1,0:T(8,128)S(1)} %fusion), channel_id=1, source_target_pairs={{0,2},{1,3},{2,4},{3,5},{4,6},{5,7},{6,8},{7,9},{8,10},{9,11},{10,... | collective-permute-start | bytes 98312
  220.9 2.6 collective-permute-start.6
  223.4 4.2 %collective-permute-start.7 = (f32[64,128]{1,0:T(8,128)S(1)}, f32[64,128]{1,0:T(8,128)S(1)}, u32[]{:S(2)}, u32[]{:S(2)}) collective-permute-start(f32[64,128]{1,0:T(8,128)S(1)} %fusion), channel_id=1, source_target_pairs={{0,4},{1,5},{2,6},{3,7},{4,8},{5,9},{6,10},{7,11},{8,12},{9,13},{1... | collective-permute-start | bytes 98312
  227.7 3.8 %collective-permute-start.8 = (f32[64,128]{1,0:T(8,128)S(1)}, f32[64,128]{1,0:T(8,128)S(1)}, u32[]{:S(2)}, u32[]{:S(2)}) collective-permute-start(f32[64,128]{1,0:T(8,128)S(1)} %fusion), channel_id=1, source_target_pairs={{0,5},{1,6},{2,7},{3,8},{4,9},{5,10},{6,11},{7,12},{8,13},{9,14},{... | collective-permute-start | bytes 98312
  231.5 1.9 collective-permute-start.9
  234.5 4.0 %collective-permute-done.9 = f32[64,128]{1,0:T(8,128)S(1)} collective-permute-done((f32[64,128]{1,0:T(8,128)S(1)}, f32[64,128]{1,0:T(8,128)S(1)}, u32[]{:S(2)}, u32[]{:S(2)}) %collective-permute-start.9) | collective-permute-done | bytes 32800
  238.6 4.2 %concatenate.156 = f32[694,128]{1,0:T(8,128)S(1)} concatenate(f32[54,128]{1,0:T(8,128)S(1)} %collective-permute-done.13, f32[64,128]{1,0:T(8,128)} %collective-permute-done.12, f32[64,128]{1,0:T(8,128)} %collective-permute-done.11, f32[64,128]{1,0:T(8,128)} %collective-permute-done.10, f32[64,128]{1,0:T(8,128)S(1)} %collective-permute-done.9, ...), dimensions={0} | concatenate | bytes 710656
  242.8 17.2 %psum.8 = f32[54,128]{1,0:T(8,128)S(1)} all-reduce(f32[54,128]{1,0:T(8,128)S(1)} %constant_dynamic-slice_fusion), channel_id=1, replica_groups=mesh['dp'=4,'space'=64] {'dp'}, use_global_device_ids=true, to_apply=%region_0.8 | all-reduce | flops 6912 | bytes 55296 | tf_op jit(solution)/shard_map/psum | solution.py:154
  (388 shorter events, 114.7 us)
Async XLA Ops:
  0.6 15.6 %copy-start.1 = (s32[1,2,26]{2,1,0:T(2,128)S(1)}, s32[1,2,26]{2,1,0:T(2,128)}, u32[]{:S(2)}) copy-start(s32[1,2,26]{2,1,0:T(2,128)} %param.125) | copy-start | bytes 628
  2.8 30.8 %collective-permute-start = (bf16[1,2,8192]{2,1,0:T(2,128)(2,1)S(1)}, bf16[1,2,8192]{2,1,0:T(2,128)(2,1)S(1)}, u32[]{:S(2)}, u32[]{:S(2)}) collective-permute-start(bf16[1,2,8192]{2,1,0:T(2,128)(2,1)S(1)} %slice.2668), channel_id=1, source_target_pairs={{0,1},{1,2},{2,3},{3,4},{4,5},{5,6},{6,7},{7,8},{8,9},{9,10},{10,1... | collective-permute-start | bytes 98312 | tf_op jit(solution)/shard_map/ppermute | solution.py:27
  4.7 28.8 %collective-permute-start.2 = (bf16[1,2,8192]{2,1,0:T(2,128)(2,1)S(1)}, bf16[1,2,8192]{2,1,0:T(2,128)(2,1)S(1)}, u32[]{:S(2)}, u32[]{:S(2)}) collective-permute-start(bf16[1,2,8192]{2,1,0:T(2,128)(2,1)S(1)} %slice.2775), channel_id=1, source_target_pairs={{0,1},{1,2},{2,3},{3,4},{4,5},{5,6},{6,7},{7,8},{8,9},{9,10},{10,1... | collective-permute-start | bytes 98312 | tf_op jit(solution)/shard_map/ppermute | solution.py:27
  8.6 25.1 %collective-permute-start.3 = (bf16[1,2,8192]{2,1,0:T(2,128)(2,1)S(1)}, bf16[1,2,8192]{2,1,0:T(2,128)(2,1)S(1)}, u32[]{:S(2)}, u32[]{:S(2)}) collective-permute-start(bf16[1,2,8192]{2,1,0:T(2,128)(2,1)S(1)} %slice.2793), channel_id=1, source_target_pairs={{1,0},{2,1},{3,2},{4,3},{5,4},{6,5},{7,6},{8,7},{9,8},{10,9},{11,1... | collective-permute-start | bytes 98312 | tf_op jit(solution)/shard_map/ppermute | solution.py:30
  10.5 23.1 %collective-permute-start.1 = (bf16[1,2,8192]{2,1,0:T(2,128)(2,1)S(1)}, bf16[1,2,8192]{2,1,0:T(2,128)(2,1)S(1)}, u32[]{:S(2)}, u32[]{:S(2)}) collective-permute-start(bf16[1,2,8192]{2,1,0:T(2,128)(2,1)S(1)} %slice.2703), channel_id=1, source_target_pairs={{1,0},{2,1},{3,2},{4,3},{5,4},{6,5},{7,6},{8,7},{9,8},{10,9},{11,1... | collective-permute-start | bytes 98312 | tf_op jit(solution)/shard_map/ppermute | solution.py:30
  22.2 10.1 %copy-start.23 = (u32[256]{0:T(256)S(1)}, u32[256]{0:T(256)}, u32[]{:S(2)}) copy-start(u32[256]{0:T(256)} %constant.1500) | copy-start | bytes 3076
  160.1 60.7 %collective-permute-start.10 = (f32[64,128]{1,0:T(8,128)S(1)}, f32[64,128]{1,0:T(8,128)}, u32[]{:S(2)}, u32[]{:S(2)}) collective-permute-start(f32[64,128]{1,0:T(8,128)S(1)} %fusion), channel_id=1, source_target_pairs={{0,7},{1,8},{2,9},{3,10},{4,11},{5,12},{6,13},{7,14},{8,15},{9,16}... | collective-permute-start | bytes 98312
  162.0 61.4 %collective-permute-start.11 = (f32[64,128]{1,0:T(8,128)S(1)}, f32[64,128]{1,0:T(8,128)}, u32[]{:S(2)}, u32[]{:S(2)}) collective-permute-start(f32[64,128]{1,0:T(8,128)S(1)} %fusion), channel_id=1, source_target_pairs={{0,8},{1,9},{2,10},{3,11},{4,12},{5,13},{6,14},{7,15},{8,16},{9,17... | collective-permute-start | bytes 98312
  166.2 61.4 %collective-permute-start.12 = (f32[64,128]{1,0:T(8,128)S(1)}, f32[64,128]{1,0:T(8,128)}, u32[]{:S(2)}, u32[]{:S(2)}) collective-permute-start(f32[64,128]{1,0:T(8,128)S(1)} %fusion), channel_id=1, source_target_pairs={{0,9},{1,10},{2,11},{3,12},{4,13},{5,14},{6,15},{7,16},{8,17},{9,1... | collective-permute-start | bytes 98312
  169.2 62.3 %collective-permute-start.4 = (f32[64,128]{1,0:T(8,128)S(1)}, f32[64,128]{1,0:T(8,128)}, u32[]{:S(2)}, u32[]{:S(2)}) collective-permute-start(f32[64,128]{1,0:T(8,128)S(1)} %fusion), channel_id=1, source_target_pairs={{0,1},{1,2},{2,3},{3,4},{4,5},{5,6},{6,7},{7,8},{8,9},{9,10},{10,1... | collective-permute-start | bytes 98312
  198.3 1.0 copy-start.22
  198.3 4.9 %copy-start = (bf16[27,128,128]{2,1,0:T(8,128)(2,1)S(1)}, bf16[27,128,128]{2,1,0:T(8,128)(2,1)}, u32[]{:S(2)}) copy-start(bf16[27,128,128]{2,1,0:T(8,128)(2,1)} %param.126) | copy-start | bytes 2654212
  199.3 4.4 %copy-start.21 = (bf16[2,8,8,8,128]{4,3,2,1,0:T(8,128)(2,1)S(1)}, bf16[2,8,8,8,128]{4,3,2,1,0:T(8,128)(2,1)}, u32[]{:S(2)}) copy-start(bf16[2,8,8,8,128]{4,3,2,1,0:T(8,128)(2,1)} %get-tuple-element.738) | copy-start | bytes 786436
  199.3 4.6 %copy-start.20 = (bf16[2,8,8,8,128]{4,3,2,1,0:T(8,128)(2,1)S(1)}, bf16[2,8,8,8,128]{4,3,2,1,0:T(8,128)(2,1)}, u32[]{:S(2)}) copy-start(bf16[2,8,8,8,128]{4,3,2,1,0:T(8,128)(2,1)} %get-tuple-element.737) | copy-start | bytes 786436
  199.3 18.1 %collective-permute-start.13 = (f32[54,128]{1,0:T(8,128)S(1)}, f32[54,128]{1,0:T(8,128)S(1)}, u32[]{:S(2)}, u32[]{:S(2)}) collective-permute-start(f32[54,128]{1,0:T(8,128)S(1)} %copy-done.22), channel_id=1, source_target_pairs={{0,10},{1,11},{2,12},{3,13},{4,14},{5,15},{6,16},{7,17},{8,18},{9,... | collective-permute-start | bytes 82952
  203.9 1.0 copy-start.17
  204.4 1.0 copy-start.16
  206.6 1.0 copy-start.9
  206.9 1.0 copy-start.8
  217.4 17.0 %collective-permute-start.5 = (f32[64,128]{1,0:T(8,128)S(1)}, f32[64,128]{1,0:T(8,128)S(1)}, u32[]{:S(2)}, u32[]{:S(2)}) collective-permute-start(f32[64,128]{1,0:T(8,128)S(1)} %fusion), channel_id=1, source_target_pairs={{0,2},{1,3},{2,4},{3,5},{4,6},{5,7},{6,8},{7,9},{8,10},{9,11},{10,... | collective-permute-start | bytes 98312
  220.9 13.6 %collective-permute-start.6 = (f32[64,128]{1,0:T(8,128)S(1)}, f32[64,128]{1,0:T(8,128)S(1)}, u32[]{:S(2)}, u32[]{:S(2)}) collective-permute-start(f32[64,128]{1,0:T(8,128)S(1)} %fusion), channel_id=1, source_target_pairs={{0,3},{1,4},{2,5},{3,6},{4,7},{5,8},{6,9},{7,10},{8,11},{9,12},{10... | collective-permute-start | bytes 98312
  223.4 11.1 %collective-permute-start.7 = (f32[64,128]{1,0:T(8,128)S(1)}, f32[64,128]{1,0:T(8,128)S(1)}, u32[]{:S(2)}, u32[]{:S(2)}) collective-permute-start(f32[64,128]{1,0:T(8,128)S(1)} %fusion), channel_id=1, source_target_pairs={{0,4},{1,5},{2,6},{3,7},{4,8},{5,9},{6,10},{7,11},{8,12},{9,13},{1... | collective-permute-start | bytes 98312
  227.7 6.8 %collective-permute-start.8 = (f32[64,128]{1,0:T(8,128)S(1)}, f32[64,128]{1,0:T(8,128)S(1)}, u32[]{:S(2)}, u32[]{:S(2)}) collective-permute-start(f32[64,128]{1,0:T(8,128)S(1)} %fusion), channel_id=1, source_target_pairs={{0,5},{1,6},{2,7},{3,8},{4,9},{5,10},{6,11},{7,12},{8,13},{9,14},{... | collective-permute-start | bytes 98312
  231.5 7.0 %collective-permute-start.9 = (f32[64,128]{1,0:T(8,128)S(1)}, f32[64,128]{1,0:T(8,128)S(1)}, u32[]{:S(2)}, u32[]{:S(2)}) collective-permute-start(f32[64,128]{1,0:T(8,128)S(1)} %fusion), channel_id=1, source_target_pairs={{0,6},{1,7},{2,8},{3,9},{4,10},{5,11},{6,12},{7,13},{8,14},{9,15},... | collective-permute-start | bytes 98312
  (14 other events, 13.8 us)
where the time goes:
time: 263 us; the launch traced here: 261 us
  blocking collectives  81.5 us (31%)
  local copies, waits for them, and re-layouts  68.6 us (26%)
  starting transfers between devices  42.1 us (16%)
  matrix products  36.2 us (14%)
  other arithmetic  25.1 us (10%)
  waiting for transfers between devices  4.08 us (2%)
  between operations  3 us (1%)
    unnamed x1, blocking collectives  64.4 us
    unnamed x10, starting transfers between devices  32.2 us
    gather x52, local copies, waits for them, and re-layouts, fill_rims(): picked = jnp.take(source, jnp.clip(local, 0, count - 1), axis=0)  29.1 us
    scatter x52, local copies, waits for them, and re-layouts, fill_rims(): padded = padded.at[whole + rim_slices(offset, extent)].set(picked)  25.9 us
    dot_general x27, matrix products, forward_each(): lax.dot_general(window, flat_g, (((0,), (0,)), ((), ())), preferred_eleme...  24.4 us
    psum x1, blocking collectives, per_device(): across_scans = lax.psum(kernel_grad, 'dp')  17.2 us
    select_n x26, other arithmetic, fill_rims(): picked = jnp.where((other >= 0)[:, None, None, None, None], picked, zero_bf)  17.2 us
    unnamed x68, local copies, waits for them, and re-layouts  7.65 us
  transfers between devices with their start and end apart: 14, of which 1 were waited for; matrix products, arithmetic and copies ran while one was open for 23% of the time, Pallas kernels for 0%

commit v1 on v0

--- a/solution.py
+++ b/solution.py
@@ -17,6 +17,12 @@
     for along_y in range(3)
     for along_z in range(3)
 ]
+
+
+def gather_and_add(block, name):
+    parts = lax.all_gather(block, name, axis=0, tiled=False)
+    total = parts.sum(axis=0)
+    return total
 
 
 def padded_2(block, sides, width):
@@ -151,7 +157,7 @@
     grad_input = jnp.where(
         active, backward_sum.reshape(count, extent, extent, extent, channels), zero_f
     ).astype(jnp.bfloat16)
-    across_scans = lax.psum(kernel_grad, "dp")
+    across_scans = gather_and_add(kernel_grad, "dp")
     shard_rows = lax.psum_scatter(across_scans, "space", scatter_dimension=0, tiled=True)
     scale_factor = 1.0 / math.sqrt(scans_count * devices * count * extent**3)
     return (response[None], grad_input[None], shard_rows * scale_factor)

time: 263 us -> 294 us (1.12)
  waiting for transfers between devices: 4.08 us -> 61.4 us
  blocking collectives: 81.5 us -> 61.1 us
  local copies, waits for them, and re-layouts: 68.6 us -> 51.3 us
  between operations: 3 us -> 16.6 us
  other arithmetic: 25.1 us -> 14.9 us
  starting transfers between devices: 42.1 us -> 46.7 us
    all_gather x0 -> x1, waiting for transfers between devices: none -> 60.1 us  [gather_and_add(): parts = lax.all_gather(block, name, axis=0, tiled=False)]
    psum x1 -> x0, blocking collectives: 17.2 us -> none  [per_device(): across_scans = lax.psum(kernel_grad, 'dp')]
    scatter x52, local copies, waits for them, and re-layouts: 25.9 us -> 9.15 us  [fill_rims(): padded = padded.at[whole + rim_slices(offset, extent)].set(picked)]
    select_n x26, other arithmetic: 17.2 us -> 2.39 us  [fill_rims(): picked = jnp.where((other >= 0)[:, None, None, None, None], picked, zero_bf)]
    unnamed x10, starting transfers between devices: 32.2 us -> 36.8 us
    reduce_sum x0 -> x1, other arithmetic: none -> 3.58 us  [gather_and_add(): total = parts.sum(axis=0)]
    unnamed x1, blocking collectives: 64.4 us -> 61.1 us
    unnamed x68 -> x85, local copies, waits for them, and re-layouts: 7.65 us -> 6.15 us
  transfers between devices with their start and end apart: 14 -> 15, of which waited for: 1 -> 2; matrix products, arithmetic and copies ran while one was open for 23% -> 11% of each run, Pallas kernels for 0% -> 0%
where the time goes in v1:
time: 294 us; the launch traced here: 290 us
  waiting for transfers between devices  61.4 us (21%)
  blocking collectives  61.1 us (21%)
  local copies, waits for them, and re-layouts  51.3 us (17%)
  starting transfers between devices  46.7 us (16%)
  matrix products  38 us (13%)
  between operations  16.6 us (6%)
  other arithmetic  14.9 us (5%)
    unnamed x1, blocking collectives  61.1 us
    all_gather x1, waiting for transfers between devices, gather_and_add(): parts = lax.all_gather(block, name, axis=0, tiled=False)  60.1 us
    unnamed x10, starting transfers between devices  36.8 us
    gather x52, local copies, waits for them, and re-layouts, fill_rims(): picked = jnp.take(source, jnp.clip(local, 0, count - 1), axis=0)  29.1 us
    dot_general x27, matrix products, forward_each(): lax.dot_general(window, flat_g, (((0,), (0,)), ((), ())), preferred_eleme...  24.4 us
    scatter x52, local copies, waits for them, and re-layouts, fill_rims(): padded = padded.at[whole + rim_slices(offset, extent)].set(picked)  9.15 us
    dot_general x27, matrix products, backward_each(): lax.dot_general(window, weight[number], (((1,), (1,)), ((), ())), preferr...  7.74 us
    unnamed x85, local copies, waits for them, and re-layouts  6.15 us
  transfers between devices with their start and end apart: 15, of which 2 were waited for; matrix products, arithmetic and copies ran while one was open for 11% of the time, Pallas kernels for 0%

profile of v1, /device:TPU:6, one launch (start us, length us, event | category | flops | bytes accessed | tf_op | source)
XLA Modules:
  0.0 290.2 jit_solution(14889620193271688456)
XLA Ops:
  9.4 1.9 collective-permute-start.2
  11.3 3.8 %collective-permute-start = (bf16[1,2,8192]{2,1,0:T(2,128)(2,1)S(1)}, bf16[1,2,8192]{2,1,0:T(2,128)(2,1)S(1)}, u32[]{:S(2)}, u32[]{:S(2)}) collective-permute-start(bf16[1,2,8192]{2,1,0:T(2,128)(2,1)S(1)} %slice.2668), channel_id=1, source_target_pairs={{0,1},{1,2},{2,3},{3,4},{4,5},{5,6},{6,7},{7,8},{8,9},{9,10},{10,1... | collective-permute-start | bytes 98312 | tf_op jit(solution)/shard_map/ppermute | solution.py:33
  15.2 1.9 collective-permute-start.3
  17.1 2.2 collective-permute-start.1
  20.6 1.9 compare_reduce_fusion
  58.2 1.4 scatter.236
  59.6 1.4 scatter.239
  62.6 1.4 fusion.182
  64.0 2.5 fusion.181
  71.3 1.4 fusion.184
  115.7 60.1 %all-gather.3.cloned.1.call-done = f32[13824,128]{1,0:T(8,128)} async-done(((f32[3456,128]{1,0:T(8,128)}), f32[13824,128]{1,0:T(8,128)}) %all-gather.3.cloned.1.call-update) | async-done | bytes 7077904 | tf_op jit(solution)/shard_map/all_gather | solution.py:23
  175.8 3.6 %reduce_sum.9 = f32[3456,128]{1,0:T(8,128)S(1)} reduce(f32[4,3456,128]{2,1,0:T(8,128)} %bitcast.753, f32[]{:T(128)} %constant.1488.clone.1), dimensions={0}, to_apply=%region_0.8 | reduce | flops 1327104 | bytes 8847364 | tf_op jit(solution)/shard_map/reduce_sum | solution.py:24
  179.4 61.1 %fusion = f32[64,128]{1,0:T(8,128)S(1)} fusion(f32[3456,128]{1,0:T(8,128)S(1)} %reduce_sum.9), kind=kCustom, calls=%all-reduce-scatter | all-reduce-scatter fusion | flops 524289 | bytes 1803264
  241.8 4.2 %collective-permute-start.11 = (f32[64,128]{1,0:T(8,128)S(1)}, f32[64,128]{1,0:T(8,128)S(1)}, u32[]{:S(2)}, u32[]{:S(2)}) collective-permute-start(f32[64,128]{1,0:T(8,128)S(1)} %fusion), channel_id=1, source_target_pairs={{0,8},{1,9},{2,10},{3,11},{4,12},{5,13},{6,14},{7,15},{8,16},{9,17... | collective-permute-start | bytes 98312
  246.1 3.9 %collective-permute-start.10 = (f32[64,128]{1,0:T(8,128)S(1)}, f32[64,128]{1,0:T(8,128)S(1)}, u32[]{:S(2)}, u32[]{:S(2)}) collective-permute-start(f32[64,128]{1,0:T(8,128)S(1)} %fusion), channel_id=1, source_target_pairs={{0,7},{1,8},{2,9},{3,10},{4,11},{5,12},{6,13},{7,14},{8,15},{9,16}... | collective-permute-start | bytes 98312
  250.0 4.3 %collective-permute-start.9 = (f32[64,128]{1,0:T(8,128)S(1)}, f32[64,128]{1,0:T(8,128)S(1)}, u32[]{:S(2)}, u32[]{:S(2)}) collective-permute-start(f32[64,128]{1,0:T(8,128)S(1)} %fusion), channel_id=1, source_target_pairs={{0,6},{1,7},{2,8},{3,9},{4,10},{5,11},{6,12},{7,13},{8,14},{9,15},... | collective-permute-start | bytes 98312
  254.3 4.8 %collective-permute-start.13 = (f32[54,128]{1,0:T(8,128)S(1)}, f32[54,128]{1,0:T(8,128)S(1)}, u32[]{:S(2)}, u32[]{:S(2)}) collective-permute-start(f32[54,128]{1,0:T(8,128)S(1)} %slice.3039), channel_id=1, source_target_pairs={{0,10},{1,11},{2,12},{3,13},{4,14},{5,15},{6,16},{7,17},{8,18},{9,... | collective-permute-start | bytes 82952
  260.7 2.1 collective-permute-start.8
  262.8 5.8 %collective-permute-start.7 = (f32[64,128]{1,0:T(8,128)S(1)}, f32[64,128]{1,0:T(8,128)S(1)}, u32[]{:S(2)}, u32[]{:S(2)}) collective-permute-start(f32[64,128]{1,0:T(8,128)S(1)} %fusion), channel_id=1, source_target_pairs={{0,4},{1,5},{2,6},{3,7},{4,8},{5,9},{6,10},{7,11},{8,12},{9,13},{1... | collective-permute-start | bytes 98312
  268.7 3.7 %collective-permute-start.6 = (f32[64,128]{1,0:T(8,128)S(1)}, f32[64,128]{1,0:T(8,128)S(1)}, u32[]{:S(2)}, u32[]{:S(2)}) collective-permute-start(f32[64,128]{1,0:T(8,128)S(1)} %fusion), channel_id=1, source_target_pairs={{0,3},{1,4},{2,5},{3,6},{4,7},{5,8},{6,9},{7,10},{8,11},{9,12},{10... | collective-permute-start | bytes 98312
  272.4 3.1 %collective-permute-start.5 = (f32[64,128]{1,0:T(8,128)S(1)}, f32[64,128]{1,0:T(8,128)S(1)}, u32[]{:S(2)}, u32[]{:S(2)}) collective-permute-start(f32[64,128]{1,0:T(8,128)S(1)} %fusion), channel_id=1, source_target_pairs={{0,2},{1,3},{2,4},{3,5},{4,6},{5,7},{6,8},{7,9},{8,10},{9,11},{10,... | collective-permute-start | bytes 98312
  275.5 3.5 %collective-permute-start.4 = (f32[64,128]{1,0:T(8,128)S(1)}, f32[64,128]{1,0:T(8,128)S(1)}, u32[]{:S(2)}, u32[]{:S(2)}) collective-permute-start(f32[64,128]{1,0:T(8,128)S(1)} %fusion), channel_id=1, source_target_pairs={{0,1},{1,2},{2,3},{3,4},{4,5},{5,6},{6,7},{7,8},{8,9},{9,10},{10,1... | collective-permute-start | bytes 98312
  279.0 2.0 select_convert_fusion
  281.0 1.7 concatenate.156
  (408 shorter events, 89.9 us)
Async XLA Ops:
  7.2 15.6 %copy-start.1 = (s32[1,2,26]{2,1,0:T(2,128)S(1)}, s32[1,2,26]{2,1,0:T(2,128)}, u32[]{:S(2)}) copy-start(s32[1,2,26]{2,1,0:T(2,128)} %param.125) | copy-start | bytes 628
  7.2 168.6 %all-gather.3.cloned.1.call-start = ((), (), s32[]{:S(2)}) async-start(), calls=%async_computation | async-start | bytes 8847360 | tf_op jit(solution)/shard_map/all_gather | solution.py:23
  9.4 26.6 %collective-permute-start.2 = (bf16[1,2,8192]{2,1,0:T(2,128)(2,1)S(1)}, bf16[1,2,8192]{2,1,0:T(2,128)(2,1)S(1)}, u32[]{:S(2)}, u32[]{:S(2)}) collective-permute-start(bf16[1,2,8192]{2,1,0:T(2,128)(2,1)S(1)} %slice.2775), channel_id=1, source_target_pairs={{0,1},{1,2},{2,3},{3,4},{4,5},{5,6},{6,7},{7,8},{8,9},{9,10},{10,1... | collective-permute-start | bytes 98312 | tf_op jit(solution)/shard_map/ppermute | solution.py:33
  11.3 24.7 %collective-permute-start = (bf16[1,2,8192]{2,1,0:T(2,128)(2,1)S(1)}, bf16[1,2,8192]{2,1,0:T(2,128)(2,1)S(1)}, u32[]{:S(2)}, u32[]{:S(2)}) collective-permute-start(bf16[1,2,8192]{2,1,0:T(2,128)(2,1)S(1)} %slice.2668), channel_id=1, source_target_pairs={{0,1},{1,2},{2,3},{3,4},{4,5},{5,6},{6,7},{7,8},{8,9},{9,10},{10,1... | collective-permute-start | bytes 98312 | tf_op jit(solution)/shard_map/ppermute | solution.py:33
  15.2 20.9 %collective-permute-start.3 = (bf16[1,2,8192]{2,1,0:T(2,128)(2,1)S(1)}, bf16[1,2,8192]{2,1,0:T(2,128)(2,1)S(1)}, u32[]{:S(2)}, u32[]{:S(2)}) collective-permute-start(bf16[1,2,8192]{2,1,0:T(2,128)(2,1)S(1)} %slice.2793), channel_id=1, source_target_pairs={{1,0},{2,1},{3,2},{4,3},{5,4},{6,5},{7,6},{8,7},{9,8},{10,9},{11,1... | collective-permute-start | bytes 98312 | tf_op jit(solution)/shard_map/ppermute | solution.py:36
  17.1 19.0 %collective-permute-start.1 = (bf16[1,2,8192]{2,1,0:T(2,128)(2,1)S(1)}, bf16[1,2,8192]{2,1,0:T(2,128)(2,1)S(1)}, u32[]{:S(2)}, u32[]{:S(2)}) collective-permute-start(bf16[1,2,8192]{2,1,0:T(2,128)(2,1)S(1)} %slice.2703), channel_id=1, source_target_pairs={{1,0},{2,1},{3,2},{4,3},{5,4},{6,5},{7,6},{8,7},{9,8},{10,9},{11,1... | collective-permute-start | bytes 98312 | tf_op jit(solution)/shard_map/ppermute | solution.py:36
  28.7 6.0 %copy-start.32 = (u32[256]{0:T(256)S(1)}, u32[256]{0:T(256)}, u32[]{:S(2)}) copy-start(u32[256]{0:T(256)} %constant.1500) | copy-start | bytes 3076
  97.1 1.2 copy-start
  97.1 2.6 copy-start.24
  97.1 2.9 copy-start.23
  98.5 1.7 copy-start.22
  107.1 1.4 copy-start.31
  107.4 1.4 copy-start.30
  107.6 1.4 copy-start.29
  240.5 22.3 %collective-permute-start.12 = (f32[64,128]{1,0:T(8,128)S(1)}, f32[64,128]{1,0:T(8,128)S(1)}, u32[]{:S(2)}, u32[]{:S(2)}) collective-permute-start(f32[64,128]{1,0:T(8,128)S(1)} %fusion), channel_id=1, source_target_pairs={{0,9},{1,10},{2,11},{3,12},{4,13},{5,14},{6,15},{7,16},{8,17},{9,1... | collective-permute-start | bytes 98312
  241.8 26.8 %collective-permute-start.11 = (f32[64,128]{1,0:T(8,128)S(1)}, f32[64,128]{1,0:T(8,128)S(1)}, u32[]{:S(2)}, u32[]{:S(2)}) collective-permute-start(f32[64,128]{1,0:T(8,128)S(1)} %fusion), channel_id=1, source_target_pairs={{0,8},{1,9},{2,10},{3,11},{4,12},{5,13},{6,14},{7,15},{8,16},{9,17... | collective-permute-start | bytes 98312
  246.1 26.3 %collective-permute-start.10 = (f32[64,128]{1,0:T(8,128)S(1)}, f32[64,128]{1,0:T(8,128)S(1)}, u32[]{:S(2)}, u32[]{:S(2)}) collective-permute-start(f32[64,128]{1,0:T(8,128)S(1)} %fusion), channel_id=1, source_target_pairs={{0,7},{1,8},{2,9},{3,10},{4,11},{5,12},{6,13},{7,14},{8,15},{9,16}... | collective-permute-start | bytes 98312
  250.0 25.5 %collective-permute-start.9 = (f32[64,128]{1,0:T(8,128)S(1)}, f32[64,128]{1,0:T(8,128)S(1)}, u32[]{:S(2)}, u32[]{:S(2)}) collective-permute-start(f32[64,128]{1,0:T(8,128)S(1)} %fusion), channel_id=1, source_target_pairs={{0,6},{1,7},{2,8},{3,9},{4,10},{5,11},{6,12},{7,13},{8,14},{9,15},... | collective-permute-start | bytes 98312
  254.3 6.4 %collective-permute-start.13 = (f32[54,128]{1,0:T(8,128)S(1)}, f32[54,128]{1,0:T(8,128)S(1)}, u32[]{:S(2)}, u32[]{:S(2)}) collective-permute-start(f32[54,128]{1,0:T(8,128)S(1)} %slice.3039), channel_id=1, source_target_pairs={{0,10},{1,11},{2,12},{3,13},{4,14},{5,15},{6,16},{7,17},{8,18},{9,... | collective-permute-start | bytes 82952
  260.7 20.3 %collective-permute-start.8 = (f32[64,128]{1,0:T(8,128)S(1)}, f32[64,128]{1,0:T(8,128)S(1)}, u32[]{:S(2)}, u32[]{:S(2)}) collective-permute-start(f32[64,128]{1,0:T(8,128)S(1)} %fusion), channel_id=1, source_target_pairs={{0,5},{1,6},{2,7},{3,8},{4,9},{5,10},{6,11},{7,12},{8,13},{9,14},{... | collective-permute-start | bytes 98312
  262.8 18.2 %collective-permute-start.7 = (f32[64,128]{1,0:T(8,128)S(1)}, f32[64,128]{1,0:T(8,128)S(1)}, u32[]{:S(2)}, u32[]{:S(2)}) collective-permute-start(f32[64,128]{1,0:T(8,128)S(1)} %fusion), channel_id=1, source_target_pairs={{0,4},{1,5},{2,6},{3,7},{4,8},{5,9},{6,10},{7,11},{8,12},{9,13},{1... | collective-permute-start | bytes 98312
  268.7 12.3 %collective-permute-start.6 = (f32[64,128]{1,0:T(8,128)S(1)}, f32[64,128]{1,0:T(8,128)S(1)}, u32[]{:S(2)}, u32[]{:S(2)}) collective-permute-start(f32[64,128]{1,0:T(8,128)S(1)} %fusion), channel_id=1, source_target_pairs={{0,3},{1,4},{2,5},{3,6},{4,7},{5,8},{6,9},{7,10},{8,11},{9,12},{10... | collective-permute-start | bytes 98312
  272.4 8.6 %collective-permute-start.5 = (f32[64,128]{1,0:T(8,128)S(1)}, f32[64,128]{1,0:T(8,128)S(1)}, u32[]{:S(2)}, u32[]{:S(2)}) collective-permute-start(f32[64,128]{1,0:T(8,128)S(1)} %fusion), channel_id=1, source_target_pairs={{0,2},{1,3},{2,4},{3,5},{4,6},{5,7},{6,8},{7,9},{8,10},{9,11},{10,... | collective-permute-start | bytes 98312
  275.5 5.5 %collective-permute-start.4 = (f32[64,128]{1,0:T(8,128)S(1)}, f32[64,128]{1,0:T(8,128)S(1)}, u32[]{:S(2)}, u32[]{:S(2)}) collective-permute-start(f32[64,128]{1,0:T(8,128)S(1)} %fusion), channel_id=1, source_target_pairs={{0,1},{1,2},{2,3},{3,4},{4,5},{5,6},{6,7},{7,8},{8,9},{9,10},{10,1... | collective-permute-start | bytes 98312
  (24 other events, 23.6 us)
Sparse Core Ops, SparseCore 0:
  97.2 78.5 all-gather.2
